TPU v7x, 32 devices: a whole 2x2x4 slice. The times are simulated.
32 devices in a mesh: seq: 8 (over z, y), head: 4 (over x, core).
Axes of the slice: x: 2, y: 2, z: 4, core: 2. Of those that a mesh axis runs over, the one named last changes fastest.
Arguments:
- tokens: bfloat16 [1024, 1024], P('seq'), may hold values from -6 to 6
- cotangent: bfloat16 [1024, 1024], P('seq'), may hold values from -6 to 6
- gate_code: int32 [2, 1024, 8], P(None, 'seq', 'head'), may hold values from 0 to 723000
- beta_code: int32 [2, 1024, 8], P(None, 'seq', 'head'), may hold values from 256 to 1024
- norm1_gain: float32 [2, 1024], replicated, may hold values from 0.5 to 1.5
- weight_in: bfloat16 [2, 1024, 6144], P(None, None, 'head'), may hold values from -0.1875 to 0.1875
- conv_weight: bfloat16 [2, 4, 4096], P(None, None, 'head'), may hold values from -3 to 3
- out_gain: float32 [2, 256], replicated, may hold values from 0.5 to 1.5
- weight_out: bfloat16 [2, 2048, 1024], P(None, 'head'), may hold values from -0.25 to 0.25
- norm2_gain: float32 [2, 1024], replicated, may hold values from 0.5 to 1.5
- weight_gate: bfloat16 [2, 1024, 2816], P(None, None, 'head'), may hold values from -0.1875 to 0.1875
- weight_up: bfloat16 [2, 1024, 2816], P(None, None, 'head'), may hold values from -0.1875 to 0.1875
- weight_down: bfloat16 [2, 2816, 1024], P(None, 'head'), may hold values from -0.21875 to 0.21875
Outputs:
- activations: bfloat16 [1024, 1024], P('seq')
- input_grad: float32 [1024, 1024], P('seq')
- grad_norm1_gain: float32 [2, 1024], replicated
- grad_weight_in: float32 [2, 1024, 6144], P(None, 'seq', 'head')
- grad_conv_weight: float32 [2, 4, 4096], P(None, None, 'head')
- grad_out_gain: float32 [2, 256], replicated
- grad_weight_out: float32 [2, 2048, 1024], P(None, 'head', 'seq')
- grad_norm2_gain: float32 [2, 1024], replicated
- grad_weight_gate: float32 [2, 1024, 2816], P(None, 'seq', 'head')
- grad_weight_up: float32 [2, 1024, 2816], P(None, 'seq', 'head')
- grad_weight_down: float32 [2, 2816, 1024], P(None, 'head', 'seq')
All inputs are finite; a program needn't handle non-finite values.
Results may differ from a plain program's by a relative error of at most 0.02.
Values sent between devices are 32-bit elements; how exact they have to be, the bound alone decides.
No kernel may reach another device: no remote copies, remote signals or barrier semaphores. Data moves between devices by JAX's collectives and lax.ppermute only.
A program may use at most 256 MiB of HBM per device.

v0:
```python
import jax
import jax.numpy as jnp
from jax import lax
from jax.sharding import PartitionSpec as P

DK = 128
DV = 256
CONV = 4
SPAN = 64
STACK_LEVELS = 2
highest = lax.Precision.HIGHEST
norm_eps = 1e-06
gate_unit = 1.0 / 1048576.0
beta_unit = 1.0 / 1024.0


def from_behind(array, axis, by):
    length = lax.axis_size(axis)
    pairs = [(i, i + by) for i in range(length) if 0 <= i + by < length]
    return lax.ppermute(array, axis, pairs)


def rms_norm(stream, gain):
    return stream * lax.rsqrt(jnp.mean(stream * stream, axis=-1, keepdims=True) + norm_eps) * gain


def unit_rows(vectors):
    return vectors * lax.rsqrt(jnp.sum(vectors * vectors, axis=-1, keepdims=True) + norm_eps)


def swiglu(gate_pre, up_pre):
    return jax.nn.silu(gate_pre) * up_pre


def post_mix(outputs, gate_z, gain):
    return rms_norm(outputs, gain) * jax.nn.silu(gate_z)


def mixer_inputs(windowed, conv_taps):
    length_total = windowed.shape[0] - (CONV - 1)
    conv_out = conv_taps[0] * windowed[CONV - 1 :]
    for tap_index in range(1, CONV):
        conv_out = (
            conv_out
            + conv_taps[tap_index]
            * windowed[CONV - 1 - tap_index : CONV - 1 - tap_index + length_total]
        )
    active = jax.nn.silu(conv_out).reshape(length_total, -1, 2 * DK + DV)
    queries = unit_rows(active[:, :, :DK]) * DK ** (-0.5)
    keys_unit = unit_rows(active[:, :, DK : 2 * DK])
    return (queries, keys_unit, active[:, :, 2 * DK :])


def span_step(carry_state, pieces):
    queries, keys_unit, values_in, logdecay, beta_rate = pieces
    block_len = queries.shape[0]
    cumulated = jnp.cumsum(logdecay, axis=0)
    cum_heads = jnp.transpose(cumulated)
    row_index = lax.broadcasted_iota(jnp.int32, (1, block_len, block_len), 1)
    col_index = lax.broadcasted_iota(jnp.int32, (1, block_len, block_len), 2)
    inclusive = row_index >= col_index
    log_ratio = jnp.where(inclusive, cum_heads[:, :, None] - cum_heads[:, None, :], 0.0)
    decay_ratio = jnp.where(inclusive, jnp.exp(log_ratio), 0.0)
    beta_heads = jnp.transpose(beta_rate)
    key_key = jnp.einsum("thd,shd->hts", keys_unit, keys_unit, precision=highest)
    strict_lower = jnp.where(
        row_index > col_index, beta_heads[:, :, None] * decay_ratio * key_key, 0.0
    )
    system = strict_lower + jnp.eye(block_len, dtype=strict_lower.dtype)[None]
    decay_all = jnp.exp(cumulated)
    right_side = jnp.concatenate(
        [beta_rate[:, :, None] * values_in, (beta_rate * decay_all)[:, :, None] * keys_unit], axis=2
    )
    right_side = jnp.transpose(right_side, (1, 0, 2))
    solved_system = lax.linalg.triangular_solve(system, right_side, left_side=True, lower=True)
    val_width = values_in.shape[2]
    new_values = solved_system[:, :, :val_width] - jnp.einsum(
        "htd,hvd->htv", solved_system[:, :, val_width:], carry_state, precision=highest
    )
    query_key = jnp.einsum("thd,shd->hts", queries, keys_unit, precision=highest)
    mixing = decay_ratio * query_key
    outputs = jnp.transpose(decay_all)[:, :, None] * jnp.einsum(
        "thd,hvd->htv", queries, carry_state, precision=highest
    )
    outputs = outputs + jnp.einsum("hts,hsv->htv", mixing, new_values, precision=highest)
    to_end = jnp.exp(cumulated[-1][None, :] - cumulated)
    new_state = jnp.exp(cumulated[-1])[:, None, None] * carry_state
    new_state = new_state + jnp.einsum(
        "hsv,shd->hvd", new_values, to_end[:, :, None] * keys_unit, precision=highest
    )
    return (new_state, jnp.transpose(outputs, (1, 0, 2)))


def delta_rule(queries, keys_unit, values_in, logdecay, beta_rate, carry_state):
    length_total = queries.shape[0]
    block_count = length_total // SPAN

    def blocks(tensor):
        return tensor.reshape((block_count, SPAN) + tensor.shape[1:])

    final_state, outputs = lax.scan(
        span_step,
        carry_state,
        (
            blocks(queries),
            blocks(keys_unit),
            blocks(values_in),
            blocks(logdecay),
            blocks(beta_rate),
        ),
    )
    return (outputs.reshape((length_total,) + outputs.shape[2:]), final_state)


def state_prefix(transfer, offset):
    all_transfer, all_offset = (
        lax.all_gather(transfer, "seq", axis=0, tiled=True),
        lax.all_gather(offset, "seq", axis=0, tiled=True),
    )
    devices = lax.axis_size("seq")
    position = lax.axis_index("seq")
    transfer_kept = all_transfer.reshape((devices,) + transfer.shape)
    offsets_all = all_offset.reshape((devices,) + offset.shape)

    def advance(index_now, carry_state):
        moved = (
            jnp.einsum("hvj,hjk->hvk", carry_state, transfer_kept[index_now], precision=highest)
            + offsets_all[index_now]
        )
        return jnp.where(index_now < position, moved, carry_state)

    incoming = lax.fori_loop(0, devices, advance, jnp.zeros_like(offset))
    return (incoming, transfer_kept)


def state_back(transfer_kept, local_grad):
    all_grad = lax.all_gather(local_grad, "seq", axis=0, tiled=True)
    devices = lax.axis_size("seq")
    position = lax.axis_index("seq")
    grads_all = all_grad.reshape((devices,) + local_grad.shape)

    def retreat(step_index, carry_state):
        index_now = devices - 1 - step_index
        moved = (
            jnp.einsum("hvj,hkj->hvk", carry_state, transfer_kept[index_now], precision=highest)
            + grads_all[index_now]
        )
        return jnp.where(index_now > position, moved, carry_state)

    outgoing = lax.fori_loop(0, devices, retreat, jnp.zeros_like(local_grad))
    return outgoing


def head_total(partial_sum):
    share = lax.psum_scatter(partial_sum, "head", scatter_dimension=1, tiled=True)
    return lax.all_gather(share, "head", axis=1, tiled=True)


def layer_forward(stream, logdecay, beta_rate, weights):
    (
        gain_one,
        weight_in,
        conv_weight,
        out_gain,
        weight_out,
        gain_two,
        weight_gate,
        weight_up,
        weight_down,
    ) = weights
    length_total = stream.shape[0]
    normed = rms_norm(stream, gain_one).astype(jnp.bfloat16)
    projected = jnp.dot(normed, weight_in, preferred_element_type=jnp.float32).reshape(
        length_total, -1, 2 * DK + 2 * DV
    )
    head_count = projected.shape[1]
    conv_input = projected[:, :, : 2 * DK + DV].reshape(length_total, -1)
    gate_z = projected[:, :, 2 * DK + DV :]
    before = from_behind(conv_input[length_total - (CONV - 1) :], "seq", 1)
    windowed = jnp.concatenate([before, conv_input], axis=0)
    conv_taps = conv_weight.astype(jnp.float32)
    queries, keys_unit, values_in = mixer_inputs(windowed, conv_taps)
    wide_values = jnp.concatenate(
        [values_in, jnp.zeros((length_total, head_count, DK), jnp.float32)], axis=2
    )
    start_state = jnp.concatenate(
        [
            jnp.zeros((head_count, DV, DK), jnp.float32),
            jnp.broadcast_to(jnp.eye(DK, dtype=jnp.float32), (head_count, DK, DK)),
        ],
        axis=1,
    )
    wide_out, wide_end = delta_rule(
        queries, keys_unit, wide_values, logdecay, beta_rate, start_state
    )
    carried = wide_out[:, :, DV:]
    incoming, transfer_kept = state_prefix(wide_end[:, DV:], wide_end[:, :DV])
    outputs = wide_out[:, :, :DV] + jnp.einsum("thd,hvd->thv", carried, incoming, precision=highest)
    gated_out = post_mix(outputs, gate_z, out_gain).reshape(length_total, -1).astype(jnp.bfloat16)
    stream_mid = stream + head_total(
        jnp.dot(gated_out, weight_out, preferred_element_type=jnp.float32)
    )
    second_normed = rms_norm(stream_mid, gain_two).astype(jnp.bfloat16)
    gate_pre = jnp.dot(second_normed, weight_gate, preferred_element_type=jnp.float32)
    up_pre = jnp.dot(second_normed, weight_up, preferred_element_type=jnp.float32)
    hidden = swiglu(gate_pre, up_pre).astype(jnp.bfloat16)
    stream_next = stream_mid + head_total(
        jnp.dot(hidden, weight_down, preferred_element_type=jnp.float32)
    )
    stored = (
        stream,
        normed,
        windowed,
        conv_taps,
        gate_z,
        queries,
        keys_unit,
        values_in,
        outputs,
        carried,
        incoming,
        transfer_kept,
        gated_out,
        stream_mid,
        second_normed,
        gate_pre,
        up_pre,
        hidden,
    )
    return (stream_next, stored)


def layer_backward(grad_stream, logdecay, beta_rate, weights, stored):
    (
        gain_one,
        weight_in,
        conv_weight,
        out_gain,
        weight_out,
        gain_two,
        weight_gate,
        weight_up,
        weight_down,
    ) = weights
    (
        stream,
        normed,
        windowed,
        conv_taps,
        gate_z,
        queries,
        keys_unit,
        values_in,
        outputs,
        carried,
        incoming,
        transfer_kept,
        gated_out,
        stream_mid,
        second_normed,
        gate_pre,
        up_pre,
        hidden,
    ) = stored
    length_total = grad_stream.shape[0]
    back_bf = grad_stream.astype(jnp.bfloat16)
    grad_down = jnp.dot(hidden.T, back_bf, preferred_element_type=jnp.float32)
    grad_hidden = jnp.dot(back_bf, weight_down.T, preferred_element_type=jnp.float32)
    _, act_pull = jax.vjp(swiglu, gate_pre, up_pre)
    grad_gate_pre, grad_up_pre = act_pull(grad_hidden)
    grad_gate_pre = grad_gate_pre.astype(jnp.bfloat16)
    grad_up_pre = grad_up_pre.astype(jnp.bfloat16)
    grad_gate = jnp.dot(second_normed.T, grad_gate_pre, preferred_element_type=jnp.float32)
    grad_up = jnp.dot(second_normed.T, grad_up_pre, preferred_element_type=jnp.float32)
    ffn_partial = jnp.dot(
        grad_gate_pre, weight_gate.T, preferred_element_type=jnp.float32
    ) + jnp.dot(grad_up_pre, weight_up.T, preferred_element_type=jnp.float32)
    grad_normed_two = lax.psum(ffn_partial, "head")
    _, norm_pull = jax.vjp(rms_norm, stream_mid, gain_two)
    grad_mid, grad_gain_two = norm_pull(grad_normed_two)
    grad_stream = grad_stream + grad_mid
    back_bf = grad_stream.astype(jnp.bfloat16)
    grad_out = jnp.dot(gated_out.T, back_bf, preferred_element_type=jnp.float32)
    grad_gated = jnp.dot(back_bf, weight_out.T, preferred_element_type=jnp.float32).reshape(
        length_total, -1, DV
    )
    _, post_pull = jax.vjp(post_mix, outputs, gate_z, out_gain)
    grad_outputs, grad_gate_z, gain_mid_part = post_pull(grad_gated)
    local_grad = jnp.einsum("thv,thd->hvd", grad_outputs, carried, precision=highest)
    outgoing = state_back(transfer_kept, local_grad)

    def core_rule(queries, keys_unit, values_in):
        return delta_rule(queries, keys_unit, values_in, logdecay, beta_rate, incoming)

    _, rule_pull = jax.vjp(core_rule, queries, keys_unit, values_in)
    grad_queries, grad_keys, grad_values = rule_pull((grad_outputs, outgoing))
    _, mix_pull = jax.vjp(mixer_inputs, windowed, conv_taps)
    grad_window, grad_conv = mix_pull((grad_queries, grad_keys, grad_values))
    from_next = from_behind(grad_window[: CONV - 1], "seq", -1)
    grad_conv_in = grad_window[CONV - 1 :] + jnp.pad(
        from_next, ((length_total - (CONV - 1), 0), (0, 0))
    )
    grad_proj = (
        jnp.concatenate([grad_conv_in.reshape(length_total, -1, 2 * DK + DV), grad_gate_z], axis=2)
        .reshape(length_total, -1)
        .astype(jnp.bfloat16)
    )
    grad_in = jnp.dot(normed.T, grad_proj, preferred_element_type=jnp.float32)
    mixer_partial = jnp.dot(grad_proj, weight_in.T, preferred_element_type=jnp.float32)
    grad_normed, grad_out_gain = lax.psum((mixer_partial, gain_mid_part), "head")
    _, norm_pull = jax.vjp(rms_norm, stream, gain_one)
    grad_prev, grad_gain_one = norm_pull(grad_normed)
    return (
        grad_stream + grad_prev,
        (
            grad_gain_one,
            grad_in,
            grad_conv,
            grad_out_gain,
            grad_out,
            grad_gain_two,
            grad_gate,
            grad_up,
            grad_down,
        ),
    )


def body(
    tokens,
    cotangent,
    gate_code,
    beta_code,
    norm1_gain,
    weight_in,
    conv_weight,
    out_gain,
    weight_out,
    norm2_gain,
    weight_gate,
    weight_up,
    weight_down,
):
    logdecay = -gate_code.astype(jnp.float32) * gate_unit
    beta_rate = beta_code.astype(jnp.float32) * beta_unit
    everything = (
        norm1_gain,
        weight_in,
        conv_weight,
        out_gain,
        weight_out,
        norm2_gain,
        weight_gate,
        weight_up,
        weight_down,
    )
    stream = tokens.astype(jnp.float32)
    kept_layers = []
    for layer_idx in range(STACK_LEVELS):
        weights = tuple((tensor[layer_idx] for tensor in everything))
        stream, stored = layer_forward(stream, logdecay[layer_idx], beta_rate[layer_idx], weights)
        kept_layers.append((weights, stored))
    activations = stream.astype(jnp.bfloat16)
    grad_stream = cotangent.astype(jnp.float32)
    large_grads = []
    small_grads = []
    for layer_idx in reversed(range(STACK_LEVELS)):
        weights, stored = kept_layers[layer_idx]
        grad_stream, layer_part = layer_backward(
            grad_stream, logdecay[layer_idx], beta_rate[layer_idx], weights, stored
        )
        large_part = (layer_part[1], layer_part[4], layer_part[6], layer_part[7], layer_part[8])
        large_grads.insert(0, large_part)
        small_grads.insert(0, (layer_part[2], layer_part[0], layer_part[3], layer_part[5]))
    large_stack = tuple(
        (
            jnp.stack([grad_group[slot_index] for grad_group in large_grads])
            for slot_index in range(5)
        )
    )
    large_stack = (
        lax.psum_scatter(large_stack[0], "seq", scatter_dimension=1, tiled=True),
        lax.psum_scatter(large_stack[1], "seq", scatter_dimension=2, tiled=True),
        lax.psum_scatter(large_stack[2], "seq", scatter_dimension=1, tiled=True),
        lax.psum_scatter(large_stack[3], "seq", scatter_dimension=1, tiled=True),
        lax.psum_scatter(large_stack[4], "seq", scatter_dimension=2, tiled=True),
    )
    small_stack = tuple(
        (
            jnp.stack([grad_group[slot_index] for grad_group in small_grads])
            for slot_index in range(4)
        )
    )
    conv_grad, gain_one_grad, out_gain_grad, gain_two_grad = lax.psum(
        (small_stack[0], small_stack[1], small_stack[2], small_stack[3]), "seq"
    )
    return (
        activations,
        grad_stream,
        gain_one_grad,
        large_stack[0],
        conv_grad,
        out_gain_grad,
        large_stack[1],
        gain_two_grad,
        large_stack[2],
        large_stack[3],
        large_stack[4],
    )


def solution(mesh):
    in_specs = (
        P("seq", None),
        P("seq", None),
        P(None, "seq", "head"),
        P(None, "seq", "head"),
        P(),
        P(None, None, "head"),
        P(None, None, "head"),
        P(),
        P(None, "head", None),
        P(),
        P(None, None, "head"),
        P(None, None, "head"),
        P(None, "head", None),
    )
    out_specs = (
        P("seq", None),
        P("seq", None),
        P(),
        P(None, "seq", "head"),
        P(None, None, "head"),
        P(),
        P(None, "head", "seq"),
        P(),
        P(None, "seq", "head"),
        P(None, "seq", "head"),
        P(None, "head", "seq"),
    )
    return jax.shard_map(body, mesh=mesh, in_specs=in_specs, out_specs=out_specs, check_vma=False)
```

profile of v0, /device:TPU:0, one launch (start us, length us, event | category | flops | bytes accessed | tf_op | source)
XLA Modules:
  0.0 1594.9 jit_solution(10691709195272504350)
XLA Ops:
  41.2 28.4 %while.210 = (s32[]{:T(128)}, f32[2,384,128]{2,1,0:T(8,128)S(1)}, f32[2,64,2,384]{3,1,0,2:T(8,128)S(1)}, f32[2,64,2]{1,2,0:T(2,128)S(1)}, f32[2,64,2]{1,2,0:T(2,...) while((s32[]{:T(128)}, f32[2,384,128]{2,1,0:T(8,128)S(1)}, ...), condition=%wide.region_5.7_spmd, body=%wide.region_3.6_spmd.sunk | while | flops 340353152 | bytes 4627117 | solution.py:101
  71.3 41.7 %all-gather.7.cloned.1.call-done = f32[16,128,128]{2,1,0:T(8,128)} async-done(((f32[2,128,128]{2,1,0:T(8,128)}), f32[16,128,128]{2,1,0:T(8,128)}) %all-gather.7.cloned.1.call-update) | async-done | bytes 1048592 | tf_op jit(solution)/shard_map/all_gather | solution.py:117
  113.0 50.5 %all-gather.9.cloned.1.call-done = f32[16,256,128]{2,1,0:T(8,128)} async-done(((f32[2,256,128]{2,1,0:T(8,128)}), f32[16,256,128]{2,1,0:T(8,128)}) %all-gather.9.cloned.1.call-update) | async-done | bytes 2097168 | tf_op jit(solution)/shard_map/all_gather | solution.py:118
  163.5 20.1 %while.216 = (s32[]{:T(128)}, f32[2,256,128]{1,2,0:T(8,128)S(1)}, s32[]{:T(128)}, f32[8,2,128,128]{3,2,1,0:T(8,128)}, f32[8,2,256,128]{3,2,1,0:T(8,128)}, /*index=5*/s32[]{:T(128)}, s32[]{:T(128)}) while((s32[]{:T(128)}, f32[2,256,128]{1,2,0:T(8,128)S(1)}, s32[]{:T(128)}, f32[8,2,128,128]{3,2,1,0:T(8,128)}, ...), condition=%wide.region_7.9_spmd.clone, body=%wide.region_6.8_spmd.clone.sunk | while | flops 100925440 | bytes 2754667 | solution.py:132
  187.0 20.2 %reduce-scatter.10.cloned.1.call-done = f32[128,256]{1,0:T(8,128)} async-done(((f32[128,1024]{1,0:T(8,128)}), f32[128,256]{1,0:T(8,128)}) %reduce-scatter.10.cloned.1.call-update) | async-done | bytes 131088 | tf_op jit(solution)/shard_map/reduce_scatter | solution.py:155
  275.9 30.3 %while.211 = (s32[]{:T(128)}, f32[2,384,128]{2,1,0:T(8,128)S(1)}, f32[2,64,2,384]{3,1,0,2:T(8,128)S(1)}, f32[2,64,2]{1,2,0:T(2,128)S(1)}, f32[2,64,2]{1,2,0:T(2,...) while((s32[]{:T(128)}, f32[2,384,128]{2,1,0:T(8,128)S(1)}, ...), condition=%wide.region_17.19_spmd, body=%wide.region_15.18_spmd.sunk | while | flops 340353152 | bytes 4627117 | solution.py:101
  307.8 41.1 %all-gather.11.cloned.1.call-done = f32[16,128,128]{2,1,0:T(8,128)} async-done(((f32[2,128,128]{2,1,0:T(8,128)}), f32[16,128,128]{2,1,0:T(8,128)}) %all-gather.11.cloned.1.call-update) | async-done | bytes 1048592 | tf_op jit(solution)/shard_map/all_gather | solution.py:117
  348.9 50.4 %all-gather.13.cloned.1.call-done = f32[16,256,128]{2,1,0:T(8,128)} async-done(((f32[2,256,128]{2,1,0:T(8,128)}), f32[16,256,128]{2,1,0:T(8,128)}) %all-gather.13.cloned.1.call-update) | async-done | bytes 2097168 | tf_op jit(solution)/shard_map/all_gather | solution.py:118
  399.3 20.0 %while.217 = (s32[]{:T(128)}, f32[2,256,128]{1,2,0:T(8,128)S(1)}, s32[]{:T(128)}, f32[8,2,128,128]{3,2,1,0:T(8,128)}, f32[8,2,256,128]{3,2,1,0:T(8,128)}, /*index=5*/s32[]{:T(128)}, s32[]{:T(128)}) while((s32[]{:T(128)}, f32[2,256,128]{1,2,0:T(8,128)S(1)}, s32[]{:T(128)}, f32[8,2,128,128]{3,2,1,0:T(8,128)}, ...), condition=%wide.region_19.21_spmd.clone, body=%wide.region_18.20_spmd.clone.sunk | while | flops 100925440 | bytes 2754667 | solution.py:132
  462.5 28.1 %all-reduce.38.cloned.1.call-done = f32[128,1024]{1,0:T(8,128)} async-done(((f32[128,1024]{1,0:T(8,128)}), f32[128,1024]{1,0:T(8,128)}) %all-reduce.38.cloned.1.call-update) | async-done | bytes 524304 | tf_op jit(solution)/shard_map/psum | solution.py:278
  492.4 23.1 %reduce-scatter.16.cloned.1.call-done = f32[128,256]{1,0:T(8,128)} async-done(((f32[128,1024]{1,0:T(8,128)}), f32[128,256]{1,0:T(8,128)}) %reduce-scatter.16.cloned.1.call-update) | async-done | bytes 131088 | tf_op jit(solution)/shard_map/reduce_scatter | solution.py:155
  535.7 39.1 %while.214 = (s32[]{:T(128)}, f32[2,256,128]{2,1,0:T(8,128)S(1)}, f32[2,2,64,64]{3,2,1,0:T(8,128)}, f32[2,64,2,1]{1,2,3,0:T(2,128)S(1)}, f32[2,64,2,1]{1,2,3,0:T...) while((s32[]{:T(128)}, f32[2,256,128]{2,1,0:T(8,128)S(1)}, ...), condition=%wide.region_31.34_spmd.clone.clone, body=%wide.region_29.33_spmd.clone.clone.sunk | while | flops 164024704 | bytes 3933053 | solution.py:101
  579.9 32.3 %while.218 = (s32[]{:T(128)}, f32[2,256,128]{1,2,0:T(8,128)}, s32[]{:T(128)}, f32[8,2,128,128]{3,2,1,0:T(8,128)}, f32[8,2,256,128]{3,2,1,0:T(8,128)}, /*index=5*/s32[]{:T(128)}, s32[]{:T(128)}, s32[]{:T(128)}, s32[]{:T(128)}) while((s32[]{:T(128)}, f32[2,256,128]{1,2,0:T(8,128)}, s32[]{:T(128)}, f32[8,2,128,128]{3,2,1,0:T(8,128)}, ...), condition=%wide.region_28.30_spmd.clone, body=%wide.region_27.29_spmd.clone.sunk | while | flops 100925448 | bytes 2754729 | solution.py:150
  615.2 43.8 %while.212 = (s32[]{:T(128)}, f32[2,256,128]{2,1,0:T(8,128)S(1)}, f32[2,64,2,128]{3,1,0,2:T(8,128)}, f32[2,64,2,128]{3,1,0,2:T(8,128)}, f32[2,64,2,256]{3,1,0,2:...) while((s32[]{:T(128)}, f32[2,256,128]{2,1,0:T(8,128)S(1)}, ...), condition=%wide.region_33.38_spmd.clone, body=%wide.region_32.37_spmd.clone.sunk | while | flops 485101568 | bytes 11272125 | solution.py:101
  690.9 33.6 %all-reduce.40.cloned.1.call-done = f32[128,1024]{1,0:T(8,128)} async-done(((f32[128,1024]{1,0:T(8,128)}), f32[128,1024]{1,0:T(8,128)}) %all-reduce.40.cloned.1.call-update) | async-done | bytes 524304 | tf_op jit(solution)/shard_map/psum | solution.py:310
  731.5 33.5 %all-reduce.42.cloned.1.call-done = f32[128,1024]{1,0:T(8,128)} async-done(((f32[128,1024]{1,0:T(8,128)}), f32[128,1024]{1,0:T(8,128)}) %all-reduce.42.cloned.1.call-update) | async-done | bytes 524304 | tf_op jit(solution)/shard_map/psum | solution.py:278
  775.5 33.5 %while.215 = (s32[]{:T(128)}, f32[2,256,128]{2,1,0:T(8,128)S(1)}, f32[2,2,64,64]{3,2,1,0:T(8,128)S(1)}, f32[2,64,2,1]{1,2,3,0:T(2,128)S(1)}, f32[2,64,2,1]{1,2,3...) while((s32[]{:T(128)}, f32[2,256,128]{2,1,0:T(8,128)S(1)}, ...), condition=%wide.region_45.50_spmd.clone.clone, body=%wide.region_43.49_spmd.clone.clone.sunk | while | flops 164024704 | bytes 3990809 | solution.py:101
  843.7 35.4 %while.213 = (s32[]{:T(128)}, f32[2,256,128]{2,1,0:T(8,128)S(1)}, f32[2,64,2,128]{3,1,0,2:T(8,128)S(1)}, f32[2,64,2,128]{3,1,0,2:T(8,128)S(1)}, f32[2,64,2,256]{...) while((s32[]{:T(128)}, f32[2,256,128]{2,1,0:T(8,128)S(1)}, ...), condition=%wide.region_47.52_spmd.clone, body=%wide.region_46.51_spmd.clone.sunk | while | flops 485101568 | bytes 8618345 | solution.py:101
  945.9 38.6 %all-reduce.31 = (f32[2,1024]{1,0:T(2,128)}, f32[2,4,1024]{2,1,0:T(4,128)}, f32[2,256]{1,0:T(2,128)}, f32[2,1024]{1,0:T(2,128)}) all-reduce(f32[2,1024]{1,0:T(2,128)S(1)} %pad_maximum_fusion.8, f32[2,4,1024]{2,1,0:T(4,128)S(1)} %pad_maximum_fusion.7, ...), channel_id=1, replica_groups=mesh['seq'=8,'head'=4] {'seq'}, use_global_device_ids=true, to_apply=%region_54.59 | all-reduce | flops 12800 | bytes 102400 | tf_op jit(solution)/shard_map/psum | solution.py:394
  986.5 46.7 %reduce-scatter.20.cloned.1.call-done = f32[2,512,128]{2,1,0:T(8,128)} async-done(((f32[2,512,1024]{2,1,0:T(8,128)}), f32[2,512,128]{2,1,0:T(8,128)}) %reduce-scatter.20.cloned.1.call-update) | async-done | bytes 524304 | tf_op jit(solution)/shard_map/reduce_scatter | solution.py:383
  1033.2 114.8 %reduce-scatter.26.cloned.1.call-done = f32[2,704,128]{2,1,0:T(8,128)} async-done(((f32[2,704,1024]{2,1,0:T(8,128)}), f32[2,704,128]{2,1,0:T(8,128)}) %reduce-scatter.26.cloned.1.call-update) | async-done | bytes 720912 | tf_op jit(solution)/shard_map/reduce_scatter | solution.py:386
  1148.0 114.5 %reduce-scatter.22.cloned.1.call-done = f32[2,128,704]{1,2,0:T(8,128)} async-done(((f32[2,1024,704]{1,2,0:T(8,128)}), f32[2,128,704]{1,2,0:T(8,128)}) %reduce-scatter.22.cloned.1.call-update) | async-done | bytes 720912 | tf_op jit(solution)/shard_map/reduce_scatter | solution.py:384
  1262.5 114.5 %reduce-scatter.24.cloned.1.call-done = f32[2,128,704]{1,2,0:T(8,128)} async-done(((f32[2,1024,704]{1,2,0:T(8,128)}), f32[2,128,704]{1,2,0:T(8,128)}) %reduce-scatter.24.cloned.1.call-update) | async-done | bytes 720912 | tf_op jit(solution)/shard_map/reduce_scatter | solution.py:385
  1377.0 211.0 %reduce-scatter.18.cloned.1.call-done = f32[2,128,1536]{2,1,0:T(8,128)} async-done(((f32[2,1024,1536]{2,1,0:T(8,128)}), f32[2,128,1536]{2,1,0:T(8,128)}) %reduce-scatter.18.cloned.1.call-update) | async-done | bytes 1572880 | tf_op jit(solution)/shard_map/reduce_scatter | solution.py:382
  (1079 shorter events, 632.4 us)
Async XLA Ops:
  7.2 105.8 %all-gather.7.cloned.1.call-start = ((), (), s32[]{:S(2)}) async-start(), calls=%async_computation.9 | async-start | bytes 1179648 | tf_op jit(solution)/shard_map/all_gather | solution.py:117
  20.6 16.1 %collective-permute-start = (f32[3,1024]{0,1:T(8,128)S(1)}, f32[3,1024]{0,1:T(8,128)S(1)}, u32[]{:S(2)}, u32[]{:S(2)}) collective-permute-start(f32[3,1024]{0,1:T(8,128)S(1)} %copy.512), channel_id=1, source_target_pairs={{0,4},{4,8},{8,12},{12,16},{16,20},{20,24},{24,28},{1,5},{5,9},{9,... | collective-permute-start | bytes 36872 | tf_op jit(solution)/shard_map/ppermute | solution.py:20
  70.4 93.2 %all-gather.9.cloned.1.call-start = ((), (), s32[]{:S(2)}) async-start(), calls=%async_computation.10 | async-start | bytes 2359296 | tf_op jit(solution)/shard_map/all_gather | solution.py:118
  71.1 136.0 %reduce-scatter.10.cloned.1.call-start = ((), (), s32[]{:S(2)}) async-start(), calls=%async_computation.11 | async-start | bytes 655360 | tf_op jit(solution)/shard_map/reduce_scatter | solution.py:155
  186.9 54.5 %reduce-scatter.12.cloned.1.call-start = ((), (), s32[]{:S(2)}) async-start(), calls=%async_computation.12 | async-start | bytes 655360 | tf_op jit(solution)/shard_map/reduce_scatter | solution.py:155
  219.1 129.8 %all-gather.11.cloned.1.call-start = ((), (), s32[]{:S(2)}) async-start(), calls=%async_computation.13 | async-start | bytes 1179648 | tf_op jit(solution)/shard_map/all_gather | solution.py:117
  248.6 477.8 %copy-start = (f32[128,1024]{1,0:T(8,128)}, f32[128,1024]{1,0:T(8,128)S(1)}, u32[]{:S(2)}) copy-start(f32[128,1024]{1,0:T(8,128)S(1)} %get-tuple-element.3414) | copy-start | bytes 1572868
  254.3 15.4 collective-permute-start.1
  306.9 92.4 %all-gather.13.cloned.1.call-start = ((), (), s32[]{:S(2)}) async-start(), calls=%async_computation.14 | async-start | bytes 2359296 | tf_op jit(solution)/shard_map/all_gather | solution.py:118
  307.7 136.2 %reduce-scatter.14.cloned.1.call-start = ((), (), s32[]{:S(2)}) async-start(), calls=%async_computation.15 | async-start | bytes 655360 | tf_op jit(solution)/shard_map/reduce_scatter | solution.py:155
  423.6 67.0 %all-reduce.38.cloned.1.call-start = ((), (), s32[]{:S(2)}) async-start(), calls=%async_computation.17 | async-start | bytes 1048576 | tf_op jit(solution)/shard_map/psum | solution.py:278
  456.5 58.9 %reduce-scatter.16.cloned.1.call-start = ((), (), s32[]{:S(2)}) async-start(), calls=%async_computation.16 | async-start | bytes 655360 | tf_op jit(solution)/shard_map/reduce_scatter | solution.py:155
  459.2 120.6 %all-gather.15.cloned.1.call-start = ((), (), s32[]{:S(2)}) async-start(), calls=%async_computation.18 | async-start | bytes 2359296 | tf_op jit(solution)/shard_map/all_gather | solution.py:137
  529.6 194.8 %all-reduce.40.cloned.1.call-start = ((), (), s32[]{:S(2)}) async-start(), calls=%async_computation.19 | async-start | bytes 1048576 | tf_op jit(solution)/shard_map/psum | solution.py:310
  671.4 14.3 collective-permute-start.2
  690.8 74.1 %all-reduce.42.cloned.1.call-start = ((), (), s32[]{:S(2)}) async-start(), calls=%async_computation.20 | async-start | bytes 1048576 | tf_op jit(solution)/shard_map/psum | solution.py:278
  731.3 91.8 %all-gather.17.cloned.1.call-start = ((), (), s32[]{:S(2)}) async-start(), calls=%async_computation.21 | async-start | bytes 2359296 | tf_op jit(solution)/shard_map/all_gather | solution.py:137
  773.3 171.3 %all-reduce.44.cloned.1.call-start = ((), (), s32[]{:S(2)}) async-start(), calls=%async_computation.22 | async-start | bytes 1048576 | tf_op jit(solution)/shard_map/psum | solution.py:310
  884.7 14.0 collective-permute-start.3
  904.8 128.5 %reduce-scatter.20.cloned.1.call-start = ((), (), s32[]{:S(2)}) async-start(), calls=%async_computation.24 | async-start | bytes 4718592 | tf_op jit(solution)/shard_map/reduce_scatter | solution.py:383
  907.6 240.4 %reduce-scatter.26.cloned.1.call-start = ((), (), s32[]{:S(2)}) async-start(), calls=%async_computation.27 | async-start | bytes 6488064 | tf_op jit(solution)/shard_map/reduce_scatter | solution.py:386
  912.7 349.8 %reduce-scatter.22.cloned.1.call-start = ((), (), s32[]{:S(2)}) async-start(), calls=%async_computation.25 | async-start | bytes 6488064 | tf_op jit(solution)/shard_map/reduce_scatter | solution.py:384
  917.8 459.2 %reduce-scatter.24.cloned.1.call-start = ((), (), s32[]{:S(2)}) async-start(), calls=%async_computation.26 | async-start | bytes 6488064 | tf_op jit(solution)/shard_map/reduce_scatter | solution.py:385
  922.8 665.1 %reduce-scatter.18.cloned.1.call-start = ((), (), s32[]{:S(2)}) async-start(), calls=%async_computation.23 | async-start | bytes 14155776 | tf_op jit(solution)/shard_map/reduce_scatter | solution.py:382
  (188 other events, 4190.7 us)
Sparse Core Ops, SparseCore 0:
  70.5 42.4 all-gather.6
  115.7 47.7 all-gather.8
  187.0 20.1 reduce-scatter.9
  219.2 22.1 reduce-scatter.11
  307.1 41.8 all-gather.10
  351.5 47.7 all-gather.12
  423.7 20.1 reduce-scatter.13
  456.6 33.9 all-reduce.37
  493.7 21.7 reduce-scatter.15
  529.8 50.0 all-gather.14
  690.9 33.4 all-reduce.39
  731.4 33.4 all-reduce.41
  773.4 49.6 all-gather.16
  904.9 34.1 all-reduce.43
  943.2 90.0 reduce-scatter.19
  1037.3 110.6 reduce-scatter.25
  1152.1 110.3 reduce-scatter.21
  1266.6 110.3 reduce-scatter.23
  1381.2 206.7 reduce-scatter.17
where the time goes:
time: 1610 us; the launch traced here: 1590 us
  waiting for transfers between devices  1020 us (63%)
  other arithmetic  197 us (12%)
  matrix products  162 us (10%)
  local copies, waits for them, and re-layouts  107 us (7%)
  blocking collectives  72.1 us (4%)
  between operations  16.9 us (1%)
    reduce_scatter x1, waiting for transfers between devices, body(): lax.psum_scatter(large_stack[0], 'seq', scatter_dimension=1, tiled=True)  211 us
    another operation x32, other arithmetic, span_step(): lax.linalg.triangular_solve(system, right_side, left_side=True, lower=True)  122 us
    reduce_scatter x1, waiting for transfers between devices, body(): lax.psum_scatter(large_stack[4], 'seq', scatter_dimension=2, tiled=True)  115 us
    reduce_scatter x1, waiting for transfers between devices, body(): lax.psum_scatter(large_stack[3], 'seq', scatter_dimension=1, tiled=True)  115 us
    reduce_scatter x1, waiting for transfers between devices, body(): lax.psum_scatter(large_stack[2], 'seq', scatter_dimension=1, tiled=True)  114 us
    all_gather x2, waiting for transfers between devices, state_prefix(): lax.all_gather(offset, 'seq', axis=0, tiled=True)  101 us
    all_gather x2, waiting for transfers between devices, state_prefix(): lax.all_gather(transfer, 'seq', axis=0, tiled=True)  82.9 us
    reduce_scatter x4, waiting for transfers between devices, head_total(): lax.psum_scatter(partial_sum, 'head', scatter_dimension=1, tiled=True)  78.4 us
  transfers between devices with their start and end apart: 23, of which 22 were waited for; matrix products, arithmetic and copies ran while one was open for 8% of the time, Pallas kernels for 0%

commit v1 on v0

--- a/solution.py
+++ b/solution.py
@@ -113,8 +113,29 @@
 
 
 def state_prefix(transfer, offset):
+
+    def _match_pieces_all(original):
+        parts_out, outcome_arr, piece_now = (
+            lax.axis_size("seq"),
+            lax.axis_index("seq"),
+            original.shape[0],
+        )
+        passed, r_now = (original, 1)
+        while r_now < parts_out:
+            passed = jnp.concatenate(
+                [
+                    passed,
+                    lax.ppermute(
+                        passed, "seq", [(b, (b - r_now) % parts_out) for b in range(parts_out)]
+                    ),
+                ],
+                0,
+            )
+            r_now = 2 * r_now
+        return jnp.roll(passed, outcome_arr * piece_now, axis=0)
+
     all_transfer, all_offset = (
-        lax.all_gather(transfer, "seq", axis=0, tiled=True),
+        _match_pieces_all(transfer),
         lax.all_gather(offset, "seq", axis=0, tiled=True),
     )
     devices = lax.axis_size("seq")

time: 1610 us -> 1560 us (0.969)
  waiting for transfers between devices: 1020 us -> 952 us
    all_gather x2 -> x0, waiting for transfers between devices: 82.9 us -> none  [state_prefix(): lax.all_gather(transfer, 'seq', axis=0, tiled=True)]
    ppermute x0 -> x6, waiting for transfers between devices: none -> 74.6 us  [_match_pieces_all(): lax.ppermute(passed, 'seq', [(b, (b - r_now) % parts_out) for b in range(...]
    all_gather x2, waiting for transfers between devices: 101 us -> 35.7 us  [state_prefix(): lax.all_gather(offset, 'seq', axis=0, tiled=True)]
  transfers between devices with their start and end apart: 23 -> 27, of which waited for: 22 -> 26; matrix products, arithmetic and copies ran while one was open for 8% -> 9% of each run, Pallas kernels for 0% -> 0%
where the time goes in v1:
time: 1560 us; the launch traced here: 1540 us
  waiting for transfers between devices  952 us (61%)
  other arithmetic  203 us (13%)
  matrix products  162 us (10%)
  local copies, waits for them, and re-layouts  106 us (7%)
  blocking collectives  72.5 us (5%)
  starting transfers between devices  28.8 us (2%)
  between operations  16.7 us (1%)
    reduce_scatter x1, waiting for transfers between devices, body(): lax.psum_scatter(large_stack[0], 'seq', scatter_dimension=1, tiled=True)  211 us
    another operation x32, other arithmetic, span_step(): lax.linalg.triangular_solve(system, right_side, left_side=True, lower=True)  122 us
    reduce_scatter x1, waiting for transfers between devices, body(): lax.psum_scatter(large_stack[4], 'seq', scatter_dimension=2, tiled=True)  115 us
    reduce_scatter x1, waiting for transfers between devices, body(): lax.psum_scatter(large_stack[2], 'seq', scatter_dimension=1, tiled=True)  114 us
    reduce_scatter x1, waiting for transfers between devices, body(): lax.psum_scatter(large_stack[3], 'seq', scatter_dimension=1, tiled=True)  114 us
    reduce_scatter x4, waiting for transfers between devices, head_total(): lax.psum_scatter(partial_sum, 'head', scatter_dimension=1, tiled=True)  81.5 us
    ppermute x6, waiting for transfers between devices, _match_pieces_all(): lax.ppermute(passed, 'seq', [(b, (b - r_now) % parts_out) for b in range(...  74.6 us
    psum x2, waiting for transfers between devices, layer_backward(): grad_normed_two = lax.psum(ffn_partial, 'head')  61.6 us
  transfers between devices with their start and end apart: 27, of which 26 were waited for; matrix products, arithmetic and copies ran while one was open for 9% of the time, Pallas kernels for 0%

profile of v1, /device:TPU:0, one launch (start us, length us, event | category | flops | bytes accessed | tf_op | source)
XLA Modules:
  0.0 1544.3 jit_solution(12526290652302533007)
XLA Ops:
  41.3 28.4 %while.210 = (s32[]{:T(128)}, f32[2,384,128]{2,1,0:T(8,128)S(1)}, f32[2,64,2,384]{3,1,0,2:T(8,128)S(1)}, f32[2,64,2]{1,2,0:T(2,128)S(1)}, f32[2,64,2]{1,2,0:T(2,...) while((s32[]{:T(128)}, f32[2,384,128]{2,1,0:T(8,128)S(1)}, ...), condition=%wide.region_5.7_spmd, body=%wide.region_3.6_spmd.sunk | while | flops 340353152 | bytes 4627117 | solution.py:101
  93.1 22.7 %collective-permute-done.3 = f32[8,128,128]{2,1,0:T(8,128)S(1)} collective-permute-done((f32[8,128,128]{2,1,0:T(8,128)S(1)}, f32[8,128,128]{2,1,0:T(8,128)S(1)}, u32[]{:S(2)}, u32[]{:S(2)}) %collective-permute-start.3) | collective-permute-done | bytes 524320 | tf_op jit(solution)/shard_map/ppermute | solution.py:128
  137.0 20.1 %while.216 = (s32[]{:T(128)}, f32[2,256,128]{1,2,0:T(8,128)S(1)}, s32[]{:T(128)}, f32[8,2,128,128]{3,2,1,0:T(8,128)}, f32[8,2,256,128]{3,2,1,0:T(8,128)}, /*index=5*/s32[]{:T(128)}, s32[]{:T(128)}) while((s32[]{:T(128)}, f32[2,256,128]{1,2,0:T(8,128)S(1)}, s32[]{:T(128)}, f32[8,2,128,128]{3,2,1,0:T(8,128)}, ...), condition=%wide.region_7.10_spmd.clone, body=%wide.region_6.9_spmd.clone.sunk | while | flops 100925440 | bytes 2754667 | solution.py:153
  160.4 21.4 %reduce-scatter.10.cloned.1.call-done = f32[128,256]{1,0:T(8,128)} async-done(((f32[128,1024]{1,0:T(8,128)}), f32[128,256]{1,0:T(8,128)}) %reduce-scatter.10.cloned.1.call-update) | async-done | bytes 131088 | tf_op jit(solution)/shard_map/reduce_scatter | solution.py:176
  250.7 30.3 %while.211 = (s32[]{:T(128)}, f32[2,384,128]{2,1,0:T(8,128)S(1)}, f32[2,64,2,384]{3,1,0,2:T(8,128)S(1)}, f32[2,64,2]{1,2,0:T(2,128)S(1)}, f32[2,64,2]{1,2,0:T(2,...) while((s32[]{:T(128)}, f32[2,384,128]{2,1,0:T(8,128)S(1)}, ...), condition=%wide.region_17.20_spmd, body=%wide.region_15.19_spmd.sunk | while | flops 340353152 | bytes 4627117 | solution.py:101
  304.7 23.3 %collective-permute-done.7 = f32[8,128,128]{2,1,0:T(8,128)} collective-permute-done((f32[8,128,128]{2,1,0:T(8,128)}, f32[8,128,128]{2,1,0:T(8,128)}, u32[]{:S(2)}, u32[]{:S(2)}) %collective-permute-start.7) | collective-permute-done | bytes 524320 | tf_op jit(solution)/shard_map/ppermute | solution.py:128
  347.4 20.0 %while.217 = (s32[]{:T(128)}, f32[2,256,128]{1,2,0:T(8,128)S(1)}, s32[]{:T(128)}, f32[8,2,128,128]{3,2,1,0:T(8,128)}, f32[8,2,256,128]{3,2,1,0:T(8,128)}, /*index=5*/s32[]{:T(128)}, s32[]{:T(128)}) while((s32[]{:T(128)}, f32[2,256,128]{1,2,0:T(8,128)S(1)}, s32[]{:T(128)}, f32[8,2,128,128]{3,2,1,0:T(8,128)}, ...), condition=%wide.region_19.22_spmd.clone, body=%wide.region_18.21_spmd.clone.sunk | while | flops 100925440 | bytes 2754667 | solution.py:153
  374.4 19.4 %reduce-scatter.14.cloned.1.call-done = f32[128,256]{1,0:T(8,128)} async-done(((f32[128,1024]{1,0:T(8,128)}), f32[128,256]{1,0:T(8,128)}) %reduce-scatter.14.cloned.1.call-update) | async-done | bytes 131088 | tf_op jit(solution)/shard_map/reduce_scatter | solution.py:176
  412.5 28.1 %all-reduce.38.cloned.1.call-done = f32[128,1024]{1,0:T(8,128)} async-done(((f32[128,1024]{1,0:T(8,128)}), f32[128,1024]{1,0:T(8,128)}) %all-reduce.38.cloned.1.call-update) | async-done | bytes 524304 | tf_op jit(solution)/shard_map/psum | solution.py:299
  442.5 23.0 %reduce-scatter.16.cloned.1.call-done = f32[128,256]{1,0:T(8,128)} async-done(((f32[128,1024]{1,0:T(8,128)}), f32[128,256]{1,0:T(8,128)}) %reduce-scatter.16.cloned.1.call-update) | async-done | bytes 131088 | tf_op jit(solution)/shard_map/reduce_scatter | solution.py:176
  485.3 39.2 %while.214 = (s32[]{:T(128)}, f32[2,256,128]{2,1,0:T(8,128)S(1)}, f32[2,2,64,64]{3,2,1,0:T(8,128)}, f32[2,64,2,1]{1,2,3,0:T(2,128)S(1)}, f32[2,64,2,1]{1,2,3,0:T...) while((s32[]{:T(128)}, f32[2,256,128]{2,1,0:T(8,128)S(1)}, ...), condition=%wide.region_31.35_spmd.clone.clone, body=%wide.region_29.34_spmd.clone.clone.sunk | while | flops 164024704 | bytes 3933053 | solution.py:101
  529.9 32.3 %while.218 = (s32[]{:T(128)}, f32[2,256,128]{1,2,0:T(8,128)}, s32[]{:T(128)}, f32[8,2,128,128]{3,2,1,0:T(8,128)}, f32[8,2,256,128]{3,2,1,0:T(8,128)}, /*index=5*/s32[]{:T(128)}, s32[]{:T(128)}, s32[]{:T(128)}, s32[]{:T(128)}) while((s32[]{:T(128)}, f32[2,256,128]{1,2,0:T(8,128)}, s32[]{:T(128)}, f32[8,2,128,128]{3,2,1,0:T(8,128)}, ...), condition=%wide.region_28.31_spmd.clone, body=%wide.region_27.30_spmd.clone.sunk | while | flops 100925448 | bytes 2754729 | solution.py:171
  565.3 43.8 %while.212 = (s32[]{:T(128)}, f32[2,256,128]{2,1,0:T(8,128)S(1)}, f32[2,64,2,128]{3,1,0,2:T(8,128)}, f32[2,64,2,128]{3,1,0,2:T(8,128)}, f32[2,64,2,256]{3,1,0,2:...) while((s32[]{:T(128)}, f32[2,256,128]{2,1,0:T(8,128)S(1)}, ...), condition=%wide.region_33.39_spmd.clone, body=%wide.region_32.38_spmd.clone.sunk | while | flops 485101568 | bytes 11272125 | solution.py:101
  641.1 33.3 %all-reduce.40.cloned.1.call-done = f32[128,1024]{1,0:T(8,128)} async-done(((f32[128,1024]{1,0:T(8,128)}), f32[128,1024]{1,0:T(8,128)}) %all-reduce.40.cloned.1.call-update) | async-done | bytes 524304 | tf_op jit(solution)/shard_map/psum | solution.py:331
  681.5 33.4 %all-reduce.42.cloned.1.call-done = f32[128,1024]{1,0:T(8,128)} async-done(((f32[128,1024]{1,0:T(8,128)}), f32[128,1024]{1,0:T(8,128)}) %all-reduce.42.cloned.1.call-update) | async-done | bytes 524304 | tf_op jit(solution)/shard_map/psum | solution.py:299
  725.6 33.5 %while.215 = (s32[]{:T(128)}, f32[2,256,128]{2,1,0:T(8,128)S(1)}, f32[2,2,64,64]{3,2,1,0:T(8,128)S(1)}, f32[2,64,2,1]{1,2,3,0:T(2,128)S(1)}, f32[2,64,2,1]{1,2,3...) while((s32[]{:T(128)}, f32[2,256,128]{2,1,0:T(8,128)S(1)}, ...), condition=%wide.region_45.51_spmd.clone.clone, body=%wide.region_43.50_spmd.clone.clone.sunk | while | flops 164024704 | bytes 3990809 | solution.py:101
  772.7 19.6 %while.219 = (s32[]{:T(128)}, f32[2,256,128]{1,2,0:T(8,128)S(1)}, s32[]{:T(128)}, f32[8,2,128,128]{3,2,1,0:T(8,128)}, f32[8,2,256,128]{3,2,1,0:T(8,128)}, /*index=5*/s32[]{:T(128)}, s32[]{:T(128)}, s32[]{:T(128)}, s32[]{:T(128)}) while((s32[]{:T(128)}, f32[2,256,128]{1,2,0:T(8,128)S(1)}, s32[]{:T(128)}, ...), condition=%wide.region_42.48_spmd.clone, body=%wide.region_41.47_spmd.clone.sunk | while | flops 100925448 | bytes 2754729 | solution.py:171
  793.3 35.4 %while.213 = (s32[]{:T(128)}, f32[2,256,128]{2,1,0:T(8,128)S(1)}, f32[2,64,2,128]{3,1,0,2:T(8,128)S(1)}, f32[2,64,2,128]{3,1,0,2:T(8,128)S(1)}, f32[2,64,2,256]{...) while((s32[]{:T(128)}, f32[2,256,128]{2,1,0:T(8,128)S(1)}, ...), condition=%wide.region_47.53_spmd.clone, body=%wide.region_46.52_spmd.clone.sunk | while | flops 485101568 | bytes 8618345 | solution.py:101
  895.5 38.6 %all-reduce.31 = (f32[2,1024]{1,0:T(2,128)}, f32[2,4,1024]{2,1,0:T(4,128)}, f32[2,256]{1,0:T(2,128)}, f32[2,1024]{1,0:T(2,128)}) all-reduce(f32[2,1024]{1,0:T(2,128)S(1)} %pad_maximum_fusion.12, f32[2,4,1024]{2,1,0:T(4,128)S(1)} %pad_maximum_fusion.11, ...), channel_id=1, replica_groups=mesh['seq'=8,'head'=4] {'seq'}, use_global_device_ids=true, to_apply=%region_54.60 | all-reduce | flops 12800 | bytes 102400 | tf_op jit(solution)/shard_map/psum | solution.py:415
  936.2 46.8 %reduce-scatter.20.cloned.1.call-done = f32[2,512,128]{2,1,0:T(8,128)} async-done(((f32[2,512,1024]{2,1,0:T(8,128)}), f32[2,512,128]{2,1,0:T(8,128)}) %reduce-scatter.20.cloned.1.call-update) | async-done | bytes 524304 | tf_op jit(solution)/shard_map/reduce_scatter | solution.py:404
  983.0 114.8 %reduce-scatter.26.cloned.1.call-done = f32[2,704,128]{2,1,0:T(8,128)} async-done(((f32[2,704,1024]{2,1,0:T(8,128)}), f32[2,704,128]{2,1,0:T(8,128)}) %reduce-scatter.26.cloned.1.call-update) | async-done | bytes 720912 | tf_op jit(solution)/shard_map/reduce_scatter | solution.py:407
  1097.8 114.5 %reduce-scatter.22.cloned.1.call-done = f32[2,128,704]{1,2,0:T(8,128)} async-done(((f32[2,1024,704]{1,2,0:T(8,128)}), f32[2,128,704]{1,2,0:T(8,128)}) %reduce-scatter.22.cloned.1.call-update) | async-done | bytes 720912 | tf_op jit(solution)/shard_map/reduce_scatter | solution.py:405
  1212.3 114.5 %reduce-scatter.24.cloned.1.call-done = f32[2,128,704]{1,2,0:T(8,128)} async-done(((f32[2,1024,704]{1,2,0:T(8,128)}), f32[2,128,704]{1,2,0:T(8,128)}) %reduce-scatter.24.cloned.1.call-update) | async-done | bytes 720912 | tf_op jit(solution)/shard_map/reduce_scatter | solution.py:406
  1326.7 210.8 %reduce-scatter.18.cloned.1.call-done = f32[2,128,1536]{2,1,0:T(8,128)} async-done(((f32[2,1024,1536]{2,1,0:T(8,128)}), f32[2,128,1536]{2,1,0:T(8,128)}) %reduce-scatter.18.cloned.1.call-update) | async-done | bytes 1572880 | tf_op jit(solution)/shard_map/reduce_scatter | solution.py:403
  (1091 shorter events, 679.6 us)
Async XLA Ops:
  7.2 129.8 %all-gather.5.cloned.1.call-start = ((), (), s32[]{:S(2)}) async-start(), calls=%async_computation.9 | async-start | bytes 2359296 | tf_op jit(solution)/shard_map/all_gather | solution.py:139
  20.7 16.1 %collective-permute-start = (f32[3,1024]{0,1:T(8,128)S(1)}, f32[3,1024]{0,1:T(8,128)S(1)}, u32[]{:S(2)}, u32[]{:S(2)}) collective-permute-start(f32[3,1024]{0,1:T(8,128)S(1)} %copy.512), channel_id=1, source_target_pairs={{0,4},{4,8},{8,12},{12,16},{16,20},{20,24},{24,28},{1,5},{5,9},{9,... | collective-permute-start | bytes 36872 | tf_op jit(solution)/shard_map/ppermute | solution.py:20
  70.5 111.4 %reduce-scatter.10.cloned.1.call-start = ((), (), s32[]{:S(2)}) async-start(), calls=%async_computation.10 | async-start | bytes 655360 | tf_op jit(solution)/shard_map/reduce_scatter | solution.py:176
  78.7 14.2 collective-permute-start.2
  92.9 22.8 %collective-permute-start.3 = (f32[8,128,128]{2,1,0:T(8,128)S(1)}, f32[8,128,128]{2,1,0:T(8,128)S(1)}, u32[]{:S(2)}, u32[]{:S(2)}) collective-permute-start(f32[8,128,128]{2,1,0:T(8,128)S(1)} %pad_maximum_fusion.7), channel_id=1, source_target_pairs={{0,16},{4,20},{8,24},{12,28},{16,0},{20,4},{24,8},{28,12},{1,17},{... | collective-permute-start | bytes 1572872 | tf_op jit(solution)/shard_map/ppermute | solution.py:128
  160.3 56.2 %reduce-scatter.12.cloned.1.call-start = ((), (), s32[]{:S(2)}) async-start(), calls=%async_computation.11 | async-start | bytes 655360 | tf_op jit(solution)/shard_map/reduce_scatter | solution.py:176
  194.2 153.3 %all-gather.7.cloned.1.call-start = ((), (), s32[]{:S(2)}) async-start(), calls=%async_computation.12 | async-start | bytes 2359296 | tf_op jit(solution)/shard_map/all_gather | solution.py:139
  229.1 15.3 collective-permute-start.4
  281.7 112.1 %reduce-scatter.14.cloned.1.call-start = ((), (), s32[]{:S(2)}) async-start(), calls=%async_computation.13 | async-start | bytes 655360 | tf_op jit(solution)/shard_map/reduce_scatter | solution.py:176
  289.7 14.2 collective-permute-start.6
  304.7 23.3 %collective-permute-start.7 = (f32[8,128,128]{2,1,0:T(8,128)}, f32[8,128,128]{2,1,0:T(8,128)}, u32[]{:S(2)}, u32[]{:S(2)}) collective-permute-start(f32[8,128,128]{2,1,0:T(8,128)} %pad_maximum_fusion.8), channel_id=1, source_target_pairs={{0,16},{4,20},{8,24},{12,28},{16,0},{20,4},{24,8},{28,12},{1,17},{... | collective-permute-start | bytes 1572872 | tf_op jit(solution)/shard_map/ppermute | solution.py:128
  371.7 69.0 %all-reduce.38.cloned.1.call-start = ((), (), s32[]{:S(2)}) async-start(), calls=%async_computation.15 | async-start | bytes 1048576 | tf_op jit(solution)/shard_map/psum | solution.py:299
  406.6 59.0 %reduce-scatter.16.cloned.1.call-start = ((), (), s32[]{:S(2)}) async-start(), calls=%async_computation.14 | async-start | bytes 655360 | tf_op jit(solution)/shard_map/reduce_scatter | solution.py:176
  409.3 120.6 %all-gather.9.cloned.1.call-start = ((), (), s32[]{:S(2)}) async-start(), calls=%async_computation.16 | async-start | bytes 2359296 | tf_op jit(solution)/shard_map/all_gather | solution.py:158
  479.7 194.8 %all-reduce.40.cloned.1.call-start = ((), (), s32[]{:S(2)}) async-start(), calls=%async_computation.17 | async-start | bytes 1048576 | tf_op jit(solution)/shard_map/psum | solution.py:331
  621.5 14.5 collective-permute-start.8
  641.1 73.9 %all-reduce.42.cloned.1.call-start = ((), (), s32[]{:S(2)}) async-start(), calls=%async_computation.18 | async-start | bytes 1048576 | tf_op jit(solution)/shard_map/psum | solution.py:299
  681.3 91.4 %all-gather.11.cloned.1.call-start = ((), (), s32[]{:S(2)}) async-start(), calls=%async_computation.19 | async-start | bytes 2359296 | tf_op jit(solution)/shard_map/all_gather | solution.py:158
  723.3 171.0 %all-reduce.44.cloned.1.call-start = ((), (), s32[]{:S(2)}) async-start(), calls=%async_computation.20 | async-start | bytes 1048576 | tf_op jit(solution)/shard_map/psum | solution.py:331
  854.4 128.6 %reduce-scatter.20.cloned.1.call-start = ((), (), s32[]{:S(2)}) async-start(), calls=%async_computation.22 | async-start | bytes 4718592 | tf_op jit(solution)/shard_map/reduce_scatter | solution.py:404
  857.2 240.5 %reduce-scatter.26.cloned.1.call-start = ((), (), s32[]{:S(2)}) async-start(), calls=%async_computation.25 | async-start | bytes 6488064 | tf_op jit(solution)/shard_map/reduce_scatter | solution.py:407
  862.3 350.0 %reduce-scatter.22.cloned.1.call-start = ((), (), s32[]{:S(2)}) async-start(), calls=%async_computation.23 | async-start | bytes 6488064 | tf_op jit(solution)/shard_map/reduce_scatter | solution.py:405
  867.4 459.3 %reduce-scatter.24.cloned.1.call-start = ((), (), s32[]{:S(2)}) async-start(), calls=%async_computation.24 | async-start | bytes 6488064 | tf_op jit(solution)/shard_map/reduce_scatter | solution.py:406
  872.5 665.1 %reduce-scatter.18.cloned.1.call-start = ((), (), s32[]{:S(2)}) async-start(), calls=%async_computation.21 | async-start | bytes 14155776 | tf_op jit(solution)/shard_map/reduce_scatter | solution.py:403
  (192 other events, 4325.0 us)
Sparse Core Ops, SparseCore 0:
  70.6 66.2 all-gather.4
  160.4 21.3 reduce-scatter.9
  194.3 22.1 reduce-scatter.11
  281.9 65.5 all-gather.6
  371.8 21.9 reduce-scatter.13
  406.7 33.9 all-reduce.37
  443.7 21.7 reduce-scatter.15
  479.8 49.9 all-gather.8
  641.2 33.2 all-reduce.39
  681.4 33.4 all-reduce.41
  723.4 49.2 all-gather.10
  854.5 34.1 all-reduce.43
  892.9 90.0 reduce-scatter.19
  987.1 110.6 reduce-scatter.25
  1101.9 110.3 reduce-scatter.21
  1216.4 110.3 reduce-scatter.23
  1330.7 206.7 reduce-scatter.17
